TPU v7x, 32 devices: a whole 2x2x4 slice. The times are simulated.
32 devices in a mesh: grp: 2 (over x), row: 8 (over z, y), col: 2 (over core).
Axes of the slice: x: 2, y: 2, z: 4, core: 2. Of those that a mesh axis runs over, the one named last changes fastest.
Arguments:
- queries: bfloat16 [128, 32, 1024], P(('grp', 'row'), 'col'), parts along dimension 0, may hold values from -4 to 4
- key_map: bfloat16 [128, 32, 1024], P(('grp', 'row'), 'col'), parts along dimension 0, may hold values from -4 to 4
- value_map: bfloat16 [128, 32, 1024], P(('grp', 'row'), 'col'), parts along dimension 0, may hold values from -4 to 4
- saved_output: bfloat16 [128, 32, 1024], P(('grp', 'row'), 'col'), parts along dimension 0, may hold values from -4 to 4, as said below
- output_grad: bfloat16 [128, 32, 1024], P(('grp', 'row'), 'col'), parts along dimension 0, may hold values from -48 to 48
- saved_logsum: float32 [128, 32, 16], P(('grp', 'row'), 'col'), parts along dimension 0, may hold values from -128 to 140, as said below
Outputs:
- query_grad: float32 [128, 32, 1024], P(('grp', 'row'), 'col'), parts along dimension 0
- key_grad: float32 [128, 32, 1024], P(('grp', 'row'), 'col'), parts along dimension 0
- value_grad: float32 [128, 32, 1024], P(('grp', 'row'), 'col'), parts along dimension 0
There are 2 independent parts, one for each index of `grp`. A program takes and returns all parts, laid end to end along the dimension named above; each array names one. Nothing has to cross between parts.
Inputs may be any that keep to these rules, and one draw needn't show every extreme that they name: `saved_output`: the attention output of these queries, keys and values over the stripes of the steps, sum over j of softmax of scores times value_map[j], rounded to bfloat16. `saved_logsum`: for each token and head, the natural logarithm of the sum of exp(scores) over the keys of its stripe.
All inputs are finite; a program needn't handle non-finite values.
Results may differ from a plain program's by a relative error of at most 0.003.
Values may be sent and summed in bfloat16 or wider, within the bound.
A program may use at most 128 MiB of HBM per device.

v0:
```python
import math
import jax
import jax.numpy as jnp
from jax import lax
from jax.sharding import PartitionSpec as P

HEADS = 16
HD = 64
SW = 8


def attention_terms(
    stripe_query, stripe_key, stripe_value, stripe_grad, stripe_logsum, stripe_delta
):
    scale = 1.0 / math.sqrt(HD)
    scores = (
        jnp.einsum("gahe,gbhe->ghab", stripe_query, stripe_key, preferred_element_type=jnp.float32)
        * scale
    )
    probs = jnp.exp(scores - jnp.swapaxes(stripe_logsum, 1, 2)[..., None])
    grad_probs = jnp.einsum(
        "gahe,gbhe->ghab", stripe_grad, stripe_value, preferred_element_type=jnp.float32
    )
    grad_scores = (probs * (grad_probs - jnp.swapaxes(stripe_delta, 1, 2)[..., None])).astype(
        jnp.bfloat16
    )
    return (probs.astype(jnp.bfloat16), grad_scores)


def query_side(grad_scores, stripe_key):
    total = jnp.einsum(
        "ghab,gbhe->gahe", grad_scores, stripe_key, preferred_element_type=jnp.float32
    )
    return total * (1.0 / math.sqrt(HD))


def key_side(probs_half, grad_scores, stripe_query, stripe_grad):
    key_total = jnp.einsum(
        "ghab,gahe->gbhe", grad_scores, stripe_query, preferred_element_type=jnp.float32
    )
    value_total = jnp.einsum(
        "ghab,gahe->gbhe", probs_half, stripe_grad, preferred_element_type=jnp.float32
    )
    return (key_total * (1.0 / math.sqrt(HD)), value_total)


def in_blocks(step, carry, arrays, size):
    length = arrays[0].shape[0]

    def turn(index, total):
        parts = tuple((lax.dynamic_slice_in_dim(array, index * size, size, 0) for array in arrays))
        return step(total, parts)

    return lax.fori_loop(0, length // size, turn, carry)


def local(queries, key_map, value_map, saved_output, output_grad, saved_logsum):
    rows, cols, width = queries.shape
    half = HEADS // 2
    split = half * HD
    tail = (half, HD)
    block = 4 * rows
    products = output_grad.astype(jnp.float32) * saved_output.astype(jnp.float32)
    delta_all = jnp.sum(products.reshape(rows, cols, HEADS, HD), axis=3)

    def row_group(values, last):
        return values.reshape((rows // SW, SW * values.shape[1]) + last)

    def column_group(values, last):
        count = values.shape[0]
        shaped = values.reshape((count, cols // SW, SW) + last)
        return jnp.swapaxes(shaped, 0, 1).reshape((cols // SW, count * SW) + last)

    def column_back(values, count):
        shaped = values.reshape((cols // SW, count, SW, -1))
        return jnp.swapaxes(shaped, 0, 1).reshape(count, cols, -1)

    full_key, full_value = (
        lax.all_gather(key_map[:, :, :split], "col", axis=1, tiled=True),
        lax.all_gather(value_map[:, :, :split], "col", axis=1, tiled=True),
    )
    wide = full_key.shape[1]
    stripe_query = row_group(queries[:, :, :split], tail)
    stripe_grad = row_group(output_grad[:, :, :split], tail)
    stripe_logsum = row_group(saved_logsum[:, :, :half], (half,))
    stripe_delta = row_group(delta_all[:, :, :half], (half,))
    stripe_key = row_group(full_key, tail)
    stripe_value = row_group(full_value, tail)
    probs_half, grad_scores = attention_terms(
        stripe_query, stripe_key, stripe_value, stripe_grad, stripe_logsum, stripe_delta
    )
    row_query_grad = query_side(grad_scores, stripe_key).reshape(rows, cols, split)
    row_key_part, row_value_part = key_side(probs_half, grad_scores, stripe_query, stripe_grad)
    row_term = jnp.concatenate(
        (row_key_part.reshape(rows, wide, split), row_value_part.reshape(rows, wide, split)), axis=2
    )
    row_sums = lax.psum_scatter(row_term, "col", scatter_dimension=1, tiled=True)
    local_key = key_map[:, :, split:]
    local_value = value_map[:, :, split:]
    column_query = column_group(queries[:, :, split:], tail)
    column_grad = column_group(output_grad[:, :, split:], tail)
    column_logsum = column_group(saved_logsum[:, :, half:], (half,))
    column_delta = column_group(delta_all[:, :, half:], (half,))

    def query_step(total, pieces):
        grouped_key = column_group(pieces[0], tail)
        grouped_value = column_group(pieces[1], tail)
        weights, gradients = attention_terms(
            column_query, grouped_key, grouped_value, column_grad, column_logsum, column_delta
        )
        return total + query_side(gradients, grouped_key)

    empty_query = jnp.zeros(column_query.shape, jnp.float32)
    every_key, every_value = (
        lax.all_gather(local_key, "row", axis=0, tiled=True),
        lax.all_gather(local_value, "row", axis=0, tiled=True),
    )
    column_total = in_blocks(query_step, empty_query, (every_key, every_value), block)

    def key_step(pieces):
        count = pieces[0].shape[0]
        grouped_key = column_group(pieces[0], tail)
        grouped_value = column_group(pieces[1], tail)
        weights, gradients = attention_terms(
            column_query, grouped_key, grouped_value, column_grad, column_logsum, column_delta
        )
        key_part, value_part = key_side(weights, gradients, column_query, column_grad)
        return jnp.concatenate(
            (column_back(key_part, count), column_back(value_part, count)), axis=2
        )

    count = rows * lax.axis_size("row")
    stacked = lax.map(
        key_step,
        (
            every_key.reshape((count // block, block) + every_key.shape[1:]),
            every_value.reshape((count // block, block) + every_value.shape[1:]),
        ),
    )
    column_sums = lax.psum_scatter(
        stacked.reshape((count,) + stacked.shape[2:]), "row", scatter_dimension=0, tiled=True
    )
    column_key_grad = column_sums[:, :, :split]
    column_value_grad = column_sums[:, :, split:]
    column_query_grad = column_back(column_total, rows)
    query_grad = jnp.concatenate((row_query_grad, column_query_grad), axis=2)
    key_grad = jnp.concatenate((row_sums[:, :, :split], column_key_grad), axis=2)
    value_grad = jnp.concatenate((row_sums[:, :, split:], column_value_grad), axis=2)
    return (query_grad, key_grad, value_grad)


def solution(mesh):
    in_specs = (
        P(("grp", "row"), "col", None),
        P(("grp", "row"), "col", None),
        P(("grp", "row"), "col", None),
        P(("grp", "row"), "col", None),
        P(("grp", "row"), "col", None),
        P(("grp", "row"), "col", None),
    )
    out_specs = (
        P(("grp", "row"), "col", None),
        P(("grp", "row"), "col", None),
        P(("grp", "row"), "col", None),
    )
    return jax.shard_map(local, mesh=mesh, in_specs=in_specs, out_specs=out_specs, check_vma=False)
```

profile of v0, /device:TPU:0, one launch (start us, length us, event | category | flops | bytes accessed | tf_op | source)
XLA Modules:
  0.0 230.9 jit_solution(451609579921056078)
XLA Ops:
  8.1 1.7 fusion.35
  9.8 1.6 fusion.33
  11.5 1.0 fusion.36
  12.5 1.0 fusion.38
  14.0 2.1 all_gather.12
  16.7 2.0 all_gather.13
  21.1 0.8 copy-done.6
  23.7 1.1 pad_maximum_fusion
  26.3 28.2 %all-gather.3.cloned.1.call-done = bf16[64,16,512]{2,1,0:T(8,128)(2,1)} async-done(((bf16[8,16,512]{2,1,0:T(8,128)(2,1)}), bf16[64,16,512]{2,1,0:T(8,128)(2,1)}) %all-gather.3.cloned.1.call-update) | async-done | bytes 1048592 | tf_op jit(solution)/shard_map/all_gather | solution.py:115
  54.5 41.1 %all-gather.5.cloned.1.call-done = bf16[64,16,512]{2,1,0:T(8,128)(2,1)} async-done(((bf16[8,16,512]{2,1,0:T(8,128)(2,1)}), bf16[64,16,512]{2,1,0:T(8,128)(2,1)}) %all-gather.5.cloned.1.call-update) | async-done | bytes 1048592 | tf_op jit(solution)/shard_map/all_gather | solution.py:116
  95.6 38.5 %while.24 = (s32[]{:T(128)}, f32[2,32,16,1024]{3,2,1,0:T(8,128)}, bf16[2,32,16,512]{3,2,1,0:T(8,128)(2,1)}, bf16[2,64,8,64]{1,3,2,0:T(8,128)(2,1)S(1)}, f32[2,64...) while((s32[]{:T(128)}, f32[2,32,16,1024]{3,2,1,0:T(8,128)}, ...), condition=%wide.region_5.6_spmd, body=%wide.region_4.5_spmd.sunk | while | flops 136577024 | bytes 35135680 | solution.py:133
  95.6 2.2 constant_dynamic-slice_fusion.6
  98.9 1.4 convolution_bitcast_fusion.3
  100.3 2.0 copy.157
  102.3 1.6 reshape.209
  103.8 2.4 %copy_bitcast_fusion.7 = f32[32,16,512]{2,1,0:T(8,128)} fusion(f32[2,32,8,512]{3,2,1,0:T(8,128)} %reshape.209), kind=kLoop, calls=%fused_computation.11.clone.1 | loop fusion | bytes 2097152 | tf_op jit(solution)/shard_map/while/body/eval_jaxpr/reshape | solution.py:76
  106.2 1.6 reshape.210
  108.0 1.6 fusion.86
  109.6 0.8 copy.159
  110.4 1.6 reshape.211
  112.0 1.3 copy_bitcast_fusion.8
  113.3 1.5 fusion.87
  114.8 2.2 constant_dynamic-slice_fusion.6
  118.1 1.4 convolution_bitcast_fusion.3
  119.5 2.0 copy.157
  121.5 1.6 reshape.209
  123.1 2.4 %copy_bitcast_fusion.7 = f32[32,16,512]{2,1,0:T(8,128)} fusion(f32[2,32,8,512]{3,2,1,0:T(8,128)} %reshape.209), kind=kLoop, calls=%fused_computation.11.clone.1 | loop fusion | bytes 2097152 | tf_op jit(solution)/shard_map/while/body/eval_jaxpr/reshape | solution.py:76
  125.5 1.6 reshape.210
  127.2 1.6 fusion.86
  128.9 0.8 copy.159
  129.7 1.6 reshape.211
  131.2 1.3 copy_bitcast_fusion.8
  132.6 1.5 fusion.87
  134.1 1.0 copy-done.7
  135.7 0.9 reshape.182
  136.6 10.4 %while.25 = (s32[]{:T(128)}, f32[2,64,8,64]{1,3,2,0:T(8,128)S(1)}, bf16[64,16,512]{2,1,0:T(8,128)(2,1)}, bf16[2,64,8,64]{3,1,2,0:T(8,128)(2,1)}, f32[2,64,8]{1,2...) while((s32[]{:T(128)}, f32[2,64,8,64]{1,3,2,0:T(8,128)S(1)}, ...), condition=%wide.region_2.0_spmd.clone, body=%wide.region_1.0_spmd.clone.sunk | while | flops 102170624 | bytes 11280569 | solution.py:54
  136.6 1.3 constant_dynamic-slice_fusion.7
  138.5 0.6 copy.162
  140.2 1.6 fusion.93
  141.8 1.3 constant_dynamic-slice_fusion.7
  143.7 0.6 copy.162
  145.4 1.6 fusion.93
  147.4 1.8 pad_maximum_fusion.1
  149.2 1.1 fusion.31
  150.2 70.5 %reduce-scatter.5.cloned.1.call-done = f32[8,16,1024]{2,1,0:T(8,128)} async-done(((f32[64,16,1024]{2,1,0:T(8,128)}), f32[8,16,1024]{2,1,0:T(8,128)}) %reduce-scatter.5.cloned.1.call-update) | async-done | bytes 524304 | tf_op jit(solution)/shard_map/reduce_scatter | solution.py:140
  220.7 1.1 fusion.32
  221.8 0.8 pad_maximum_fusion.3
  222.6 0.8 pad_maximum_fusion.2
  (94 shorter events, 13.6 us)
Async XLA Ops:
  8.0 11.0 %copy-start.10 = (bf16[8,16,1024]{2,1,0:T(8,128)(2,1)S(1)}, bf16[8,16,1024]{2,1,0:T(8,128)(2,1)}, u32[]{:S(2)}) copy-start(bf16[8,16,1024]{2,1,0:T(8,128)(2,1)} %param.14) | copy-start | bytes 786436
  8.0 11.4 %copy-start.11 = (bf16[8,16,1024]{2,1,0:T(8,128)(2,1)S(1)}, bf16[8,16,1024]{2,1,0:T(8,128)(2,1)}, u32[]{:S(2)}) copy-start(bf16[8,16,1024]{2,1,0:T(8,128)(2,1)} %param.13) | copy-start | bytes 786436
  8.0 46.5 %all-gather.3.cloned.1.call-start = ((), (), s32[]{:S(2)}) async-start(), calls=%async_computation.2 | async-start | bytes 1179648 | tf_op jit(solution)/shard_map/all_gather | solution.py:115
  9.8 85.8 %all-gather.5.cloned.1.call-start = ((), (), s32[]{:S(2)}) async-start(), calls=%async_computation.3 | async-start | bytes 1179648 | tf_op jit(solution)/shard_map/all_gather | solution.py:116
  11.5 137.7 %reduce-scatter.3.cloned.1.call-start = ((), (), s32[]{:S(2)}) async-start(), calls=%async_computation.4 | async-start | bytes 1572864 | tf_op jit(solution)/shard_map/reduce_scatter | solution.py:97
  16.7 4.3 %copy-start.8 = (bf16[256,8,64]{0,2,1:T(8,128)(2,1)}, bf16[256,8,64]{0,2,1:T(8,128)(2,1)S(1)}, u32[]{:S(2)}) copy-start(bf16[256,8,64]{0,2,1:T(8,128)(2,1)S(1)} %copy.102) | copy-start | bytes 786436
  21.0 0.8 copy-start.6
  24.8 196.0 %reduce-scatter.5.cloned.1.call-start = ((), (), s32[]{:S(2)}) async-start(), calls=%async_computation.5 | async-start | bytes 4718592 | tf_op jit(solution)/shard_map/reduce_scatter | solution.py:140
  25.7 69.9 %copy-start.3 = (bf16[2,64,8,64]{3,1,2,0:T(8,128)(2,1)}, bf16[2,64,8,64]{3,1,2,0:T(8,128)(2,1)S(1)}, u32[]{:S(2)}) copy-start(bf16[2,64,8,64]{3,1,2,0:T(8,128)(2,1)S(1)} %get-tuple-element.411) | copy-start | bytes 393220
  25.7 69.9 %copy-start.5 = (bf16[2,64,8,64]{3,1,2,0:T(8,128)(2,1)}, bf16[2,64,8,64]{3,1,2,0:T(8,128)(2,1)S(1)}, u32[]{:S(2)}) copy-start(bf16[2,64,8,64]{3,1,2,0:T(8,128)(2,1)S(1)} %get-tuple-element.408) | copy-start | bytes 393220
  95.6 3.3 %copy-start.1 = (bf16[2,64,8,64]{1,3,2,0:T(8,128)(2,1)}, bf16[2,64,8,64]{1,3,2,0:T(8,128)(2,1)S(1)}, u32[]{:S(2)}) copy-start(bf16[2,64,8,64]{1,3,2,0:T(8,128)(2,1)S(1)} %get-tuple-element.462) | copy-start | bytes 393220 | tf_op jit(solution)/shard_map/while
  110.4 2.9 %copy-start = (f32[32,16,512]{2,1,0:T(8,128)S(1)}, f32[32,16,512]{2,1,0:T(8,128)}, u32[]{:S(2)}) copy-start(f32[32,16,512]{2,1,0:T(8,128)} %copy_bitcast_fusion.7) | copy-start | bytes 3145732 | tf_op jit(solution)/shard_map/while
  112.0 2.9 %copy-start.2 = (bf16[2,64,8,64]{1,3,2,0:T(8,128)(2,1)S(1)}, bf16[2,64,8,64]{1,3,2,0:T(8,128)(2,1)}, u32[]{:S(2)}) copy-start(bf16[2,64,8,64]{1,3,2,0:T(8,128)(2,1)} %copy-done.1) | copy-start | bytes 393220 | tf_op jit(solution)/shard_map/while
  114.8 3.3 %copy-start.1 = (bf16[2,64,8,64]{1,3,2,0:T(8,128)(2,1)}, bf16[2,64,8,64]{1,3,2,0:T(8,128)(2,1)S(1)}, u32[]{:S(2)}) copy-start(bf16[2,64,8,64]{1,3,2,0:T(8,128)(2,1)S(1)} %get-tuple-element.462) | copy-start | bytes 393220 | tf_op jit(solution)/shard_map/while
  129.6 2.9 %copy-start = (f32[32,16,512]{2,1,0:T(8,128)S(1)}, f32[32,16,512]{2,1,0:T(8,128)}, u32[]{:S(2)}) copy-start(f32[32,16,512]{2,1,0:T(8,128)} %copy_bitcast_fusion.7) | copy-start | bytes 3145732 | tf_op jit(solution)/shard_map/while
  131.2 2.8 %copy-start.2 = (bf16[2,64,8,64]{1,3,2,0:T(8,128)(2,1)S(1)}, bf16[2,64,8,64]{1,3,2,0:T(8,128)(2,1)}, u32[]{:S(2)}) copy-start(bf16[2,64,8,64]{1,3,2,0:T(8,128)(2,1)} %copy-done.1) | copy-start | bytes 393220 | tf_op jit(solution)/shard_map/while
  134.0 1.0 copy-start.7
  134.0 1.1 copy-start.9
  134.0 2.5 %copy-start.4 = (bf16[2,64,8,64]{3,1,2,0:T(8,128)(2,1)S(1)}, bf16[2,64,8,64]{3,1,2,0:T(8,128)(2,1)}, u32[]{:S(2)}) copy-start(bf16[2,64,8,64]{3,1,2,0:T(8,128)(2,1)} %copy-done.3) | copy-start | bytes 393220
Sparse Core Ops, SparseCore 0:
  11.6 42.9 all-gather.2
  56.6 38.8 all-gather.4
Sparse Core Ops, SparseCore 1:
  24.8 11.1 reduce-scatter.2
  134.2 86.5 reduce-scatter.4
where the time goes:
time: 232 us; the launch traced here: 231 us
  waiting for transfers between devices  140 us (60%)
  local copies, waits for them, and re-layouts  49.9 us (22%)
  between operations  15.8 us (7%)
  matrix products  12.7 us (5%)
  other arithmetic  7.9 us (3%)
  blocking collectives  4.08 us (2%)
    reduce_scatter x1, waiting for transfers between devices, local(): lax.psum_scatter(stacked.reshape((count,) + stacked.shape[2:]), 'row', sc...  70.5 us
    all_gather x1, waiting for transfers between devices, local(): lax.all_gather(local_value, 'row', axis=0, tiled=True)  41.1 us
    all_gather x1, waiting for transfers between devices, local(): lax.all_gather(local_key, 'row', axis=0, tiled=True)  28.2 us
    reshape x5, local copies, waits for them, and re-layouts, column_back(): return jnp.swapaxes(shaped, 0, 1).reshape(count, cols, -1)  7.5 us
    reshape x12, local copies, waits for them, and re-layouts, column_group(): shaped = values.reshape((count, cols // SW, SW) + last)  7.02 us
    reshape x5, local copies, waits for them, and re-layouts, column_back(): shaped = values.reshape((cols // SW, count, SW, -1))  6.37 us
  transfers between devices with their start and end apart: 4, of which 3 were waited for; matrix products, arithmetic and copies ran while one was open for 28% of the time, Pallas kernels for 0%

commit v1 on v0

--- a/solution.py
+++ b/solution.py
@@ -1,3 +1,4 @@
+import functools
 import math
 import jax
 import jax.numpy as jnp
@@ -7,6 +8,27 @@
 HEADS = 16
 HD = 64
 SW = 8
+
+
+def resolve_unit(x_in, dev_axis):
+    n_chips = jax.lax.axis_size(dev_axis)
+    block_list = [(m, (m + 1) % n_chips) for m in range(n_chips)]
+    vals = [(m, (m - 1) % n_chips) for m in range(n_chips)]
+    before, y = ([x_in], [x_in])
+    for _ in range(n_chips // 2):
+        before.append(jax.lax.ppermute(before[-1], dev_axis, block_list))
+    num = 0
+    while num < (n_chips - 1) // 2:
+        y.append(jax.lax.ppermute(y[-1], dev_axis, vals))
+        num += 1
+    return jnp.roll(
+        jnp.concatenate([*before[::-1], *y[1:]], axis=0),
+        shift=(jax.lax.axis_index(dev_axis) - n_chips // 2) * x_in.shape[0],
+        axis=0,
+    )
+
+
+view_the_ratios = functools.partial(resolve_unit, dev_axis="row")
 
 
 def attention_terms(
@@ -113,7 +135,7 @@
     empty_query = jnp.zeros(column_query.shape, jnp.float32)
     every_key, every_value = (
         lax.all_gather(local_key, "row", axis=0, tiled=True),
-        lax.all_gather(local_value, "row", axis=0, tiled=True),
+        view_the_ratios(local_value),
     )
     column_total = in_blocks(query_step, empty_query, (every_key, every_value), block)
 

time: 232 us -> 209 us (0.901)
  waiting for transfers between devices: 140 us -> 87 us
  starting transfers between devices: 0.35 us -> 16.3 us
  local copies, waits for them, and re-layouts: 49.9 us -> 64.3 us
    all_gather x1 -> x0, waiting for transfers between devices: 41.1 us -> none  [local(): lax.all_gather(local_value, 'row', axis=0, tiled=True)]
    all_gather x1, waiting for transfers between devices: 28.2 us -> 0.01 us  [local(): lax.all_gather(local_key, 'row', axis=0, tiled=True)]
    ppermute x0 -> x7, waiting for transfers between devices: none -> 16.3 us  [the longest x4 14.6 us: resolve_unit(): before.append(jax.lax.ppermute(before[-1], dev_axis, block_list))]
    ppermute x0 -> x7, starting transfers between devices: none -> 16 us  [the longest x3 15.9 us: resolve_unit(): y.append(jax.lax.ppermute(y[-1], dev_axis, vals))]
    unnamed x18 -> x46, local copies, waits for them, and re-layouts: 1.88 us -> 13.4 us
  transfers between devices with their start and end apart: 4 -> 10, of which waited for: 3 -> 5; matrix products, arithmetic and copies ran while one was open for 28% -> 36% of each run, Pallas kernels for 0% -> 0%
where the time goes in v1:
time: 209 us; the launch traced here: 208 us
  waiting for transfers between devices  87 us (42%)
  local copies, waits for them, and re-layouts  64.3 us (31%)
  starting transfers between devices  16.3 us (8%)
  between operations  16.1 us (8%)
  matrix products  12.8 us (6%)
  other arithmetic  7.11 us (3%)
  blocking collectives  3.98 us (2%)
    reduce_scatter x1, waiting for transfers between devices, local(): lax.psum_scatter(stacked.reshape((count,) + stacked.shape[2:]), 'row', sc...  70.6 us
    ppermute x3, starting transfers between devices, resolve_unit(): y.append(jax.lax.ppermute(y[-1], dev_axis, vals))  15.9 us
    ppermute x4, waiting for transfers between devices, resolve_unit(): before.append(jax.lax.ppermute(before[-1], dev_axis, block_list))  14.6 us
    unnamed x46, local copies, waits for them, and re-layouts  13.4 us
    reshape x5, local copies, waits for them, and re-layouts, column_back(): return jnp.swapaxes(shaped, 0, 1).reshape(count, cols, -1)  7.39 us
    reshape x5, local copies, waits for them, and re-layouts, column_back(): shaped = values.reshape((cols // SW, count, SW, -1))  6.08 us
    reshape x12, local copies, waits for them, and re-layouts, column_group(): shaped = values.reshape((count, cols // SW, SW) + last)  4.8 us
    transpose x3, local copies, waits for them, and re-layouts, key_side(): jnp.einsum('ghab,gahe->gbhe', probs_half, stripe_grad, preferred_element_...  4.44 us
  transfers between devices with their start and end apart: 10, of which 5 were waited for; matrix products, arithmetic and copies ran while one was open for 36% of the time, Pallas kernels for 0%

profile of v1, /device:TPU:0, one launch (start us, length us, event | category | flops | bytes accessed | tf_op | source)
XLA Modules:
  0.0 207.9 jit_solution(8476054584824247530)
XLA Ops:
  8.0 1.6 slice.57
  9.6 6.0 %collective-permute-start.4 = (bf16[8,16,512]{2,1,0:T(8,128)(2,1)}, bf16[8,16,512]{2,1,0:T(8,128)(2,1)}, u32[]{:S(2)}, u32[]{:S(2)}) collective-permute-start(bf16[8,16,512]{2,1,0:T(8,128)(2,1)} %slice.57), channel_id=1, source_target_pairs={{0,14},{2,0},{4,2},{6,4},{8,6},{10,8},{12,10},{14,12},{1,15},{3,1}... | collective-permute-start | bytes 393224 | tf_op jit(solution)/shard_map/ppermute | solution.py:22
  15.6 1.6 fusion.35
  17.4 1.0 fusion.38
  19.2 1.0 fusion.36
  20.8 2.0 all_gather.9
  27.0 10.5 %collective-permute-done.1 = bf16[8,16,512]{2,1,0:T(8,128)(2,1)S(1)} collective-permute-done((bf16[8,16,512]{2,1,0:T(8,128)(2,1)}, bf16[8,16,512]{2,1,0:T(8,128)(2,1)S(1)}, u32[]{:S(2)}, u32[]{:S(2)}) %collective-permute-start.1) | collective-permute-done | bytes 131104 | tf_op jit(solution)/shard_map/ppermute | solution.py:19
  37.5 1.1 fusion.25
  38.6 4.8 %collective-permute-start.5 = (bf16[8,16,512]{2,1,0:T(8,128)(2,1)}, bf16[8,16,512]{2,1,0:T(8,128)(2,1)S(1)}, u32[]{:S(2)}, u32[]{:S(2)}) collective-permute-start(bf16[8,16,512]{2,1,0:T(8,128)(2,1)} %collective-permute-done.4), channel_id=1, source_target_pairs={{0,14},{2,0},{4,2},{6,4},{8,6},{10,8},{12,10},{14,12},{1,15},{3,1}... | collective-permute-start | bytes 393224 | tf_op jit(solution)/shard_map/ppermute | solution.py:22
  43.3 2.0 collective-permute-done.2
  45.3 1.1 convolution_bitcast_fusion.1
  47.2 1.8 collective-permute-done.5
  48.9 5.1 %collective-permute-start.6 = (bf16[8,16,512]{2,1,0:T(8,128)(2,1)S(1)}, bf16[8,16,512]{2,1,0:T(8,128)(2,1)S(1)}, u32[]{:S(2)}, u32[]{:S(2)}) collective-permute-start(bf16[8,16,512]{2,1,0:T(8,128)(2,1)S(1)} %collective-permute-done.5), channel_id=1, source_target_pairs={{0,14},{2,0},{4,2},{6,4},{8,6},{10,8},{12,10},{14,12},{1,15},{3,1}... | collective-permute-start | bytes 393224 | tf_op jit(solution)/shard_map/ppermute | solution.py:22
  54.1 2.1 collective-permute-done.3
  58.0 0.9 constant_dynamic-update-slice_fusion.12
  59.0 0.9 constant_dynamic-update-slice_fusion.11
  63.7 1.4 copy-done.16
  65.1 2.0 all_gather.10
  67.3 1.0 fusion.26
  70.1 1.2 pad_maximum_fusion
  71.5 1.6 constant_dynamic-update-slice_fusion.2
  74.4 2.3 %constant_dynamic-slice_fusion.4 = bf16[64,16,512]{2,1,0:T(8,128)(2,1)} fusion(bf16[128,16,512]{2,1,0:T(8,128)(2,1)} %constant_dynamic-update-slice_fusion, s32[]{:T(128)S(6)} %select_n.22), kind=kLoop, calls=%fused_computation.74 | loop fusion | bytes 2097156 | tf_op jit(solution)/shard_map/jit(_roll_dynamic)/dynamic_slice | solution.py:24
  76.7 35.8 %while.24 = (s32[]{:T(128)}, f32[2,32,16,1024]{3,2,1,0:T(8,128)}, bf16[2,32,16,512]{3,2,1,0:T(8,128)(2,1)}, bf16[2,64,8,64]{1,3,2,0:T(8,128)(2,1)S(1)}, f32[2,64...) while((s32[]{:T(128)}, f32[2,32,16,1024]{3,2,1,0:T(8,128)}, ...), condition=%wide.region_5.6_spmd, body=%wide.region_4.5_spmd.sunk | while | flops 136577024 | bytes 37232860 | solution.py:155
  76.7 2.2 %constant_dynamic-slice_fusion.7 = (bf16[1,32,16,512]{3,2,1,0:T(8,128)(2,1)}, bf16[1,32,16,512]{3,2,1,0:T(8,128)(2,1)S(1)}) fusion(bf16[2,32,16,512]{3,2,1,0:T(8,128)(2,1)} %get-tuple-element.464, s32[]{:T(128)S(6)} %copy.188, bf16[2,32,16,512]{3,2,1,0:T(8,128)(2,1)} %get-tuple-element.461), kind=kLoop, calls=%fused_computation.17.clone.1 | loop fusion | bytes 2097156 | tf_op jit(solution)/shard_map/while/body/jit(dynamic_index_in_dim)/dynamic_slice | solution.py:155
  80.1 1.3 convolution_bitcast_fusion.3
  81.4 2.0 copy.157
  83.4 1.5 reshape.209
  84.9 2.4 %copy_bitcast_fusion.7 = f32[32,16,512]{2,1,0:T(8,128)} fusion(f32[2,32,8,512]{3,2,1,0:T(8,128)} %reshape.209), kind=kLoop, calls=%fused_computation.11.clone.1 | loop fusion | bytes 2097152 | tf_op jit(solution)/shard_map/while/body/eval_jaxpr/reshape | solution.py:98
  87.9 1.6 fusion.86
  90.3 1.5 reshape.211
  91.8 1.3 copy_bitcast_fusion.8
  93.1 1.5 fusion.87
  94.6 2.2 %constant_dynamic-slice_fusion.7 = (bf16[1,32,16,512]{3,2,1,0:T(8,128)(2,1)}, bf16[1,32,16,512]{3,2,1,0:T(8,128)(2,1)S(1)}) fusion(bf16[2,32,16,512]{3,2,1,0:T(8,128)(2,1)} %get-tuple-element.464, s32[]{:T(128)S(6)} %copy.188, bf16[2,32,16,512]{3,2,1,0:T(8,128)(2,1)} %get-tuple-element.461), kind=kLoop, calls=%fused_computation.17.clone.1 | loop fusion | bytes 2097156 | tf_op jit(solution)/shard_map/while/body/jit(dynamic_index_in_dim)/dynamic_slice | solution.py:155
  97.9 1.3 convolution_bitcast_fusion.3
  99.2 2.0 copy.157
  101.3 1.5 reshape.209
  102.7 2.4 %copy_bitcast_fusion.7 = f32[32,16,512]{2,1,0:T(8,128)} fusion(f32[2,32,8,512]{3,2,1,0:T(8,128)} %reshape.209), kind=kLoop, calls=%fused_computation.11.clone.1 | loop fusion | bytes 2097152 | tf_op jit(solution)/shard_map/while/body/eval_jaxpr/reshape | solution.py:98
  105.8 1.6 fusion.86
  108.2 1.5 reshape.211
  109.7 1.3 copy_bitcast_fusion.8
  111.0 1.5 fusion.87
  112.5 1.0 copy-done.9
  115.0 9.3 %while.25 = (s32[]{:T(128)}, f32[2,64,8,64]{1,3,2,0:T(8,128)S(1)}, bf16[64,16,512]{2,1,0:T(8,128)(2,1)}, bf16[2,64,8,64]{3,1,2,0:T(8,128)(2,1)}, f32[2,64,8]{1,2...) while((s32[]{:T(128)}, f32[2,64,8,64]{1,3,2,0:T(8,128)S(1)}, ...), condition=%wide.region_2.3_spmd.clone, body=%wide.region_1.0_spmd.clone.sunk | while | flops 102170624 | bytes 11804885 | solution.py:76
  115.0 1.3 constant_dynamic-slice_fusion.8
  119.7 1.3 constant_dynamic-slice_fusion.8
  126.1 1.1 fusion.31
  127.2 70.6 %reduce-scatter.5.cloned.1.call-done = f32[8,16,1024]{2,1,0:T(8,128)} async-done(((f32[64,16,1024]{2,1,0:T(8,128)}), f32[8,16,1024]{2,1,0:T(8,128)}) %reduce-scatter.5.cloned.1.call-update) | async-done | bytes 524304 | tf_op jit(solution)/shard_map/reduce_scatter | solution.py:162
  197.8 1.1 fusion.32
  (144 shorter events, 31.9 us)
Async XLA Ops:
  8.0 68.7 %all-gather.2.cloned.1.call-start = ((), (), s32[]{:S(2)}) async-start(), calls=%async_computation.2 | async-start | bytes 1179648 | tf_op jit(solution)/shard_map/all_gather | solution.py:137
  9.6 29.0 %collective-permute-start.4 = (bf16[8,16,512]{2,1,0:T(8,128)(2,1)}, bf16[8,16,512]{2,1,0:T(8,128)(2,1)}, u32[]{:S(2)}, u32[]{:S(2)}) collective-permute-start(bf16[8,16,512]{2,1,0:T(8,128)(2,1)} %slice.57), channel_id=1, source_target_pairs={{0,14},{2,0},{4,2},{6,4},{8,6},{10,8},{12,10},{14,12},{1,15},{3,1}... | collective-permute-start | bytes 393224 | tf_op jit(solution)/shard_map/ppermute | solution.py:22
  15.6 10.3 %collective-permute-start = (bf16[8,16,512]{2,1,0:T(8,128)(2,1)}, bf16[8,16,512]{2,1,0:T(8,128)(2,1)}, u32[]{:S(2)}, u32[]{:S(2)}) collective-permute-start(bf16[8,16,512]{2,1,0:T(8,128)(2,1)} %slice.57), channel_id=1, source_target_pairs={{0,2},{2,4},{4,6},{6,8},{8,10},{10,12},{12,14},{14,0},{1,3},{3,5},... | collective-permute-start | bytes 393224 | tf_op jit(solution)/shard_map/ppermute | solution.py:19
  17.3 108.8 %reduce-scatter.3.cloned.1.call-start = ((), (), s32[]{:S(2)}) async-start(), calls=%async_computation.3 | async-start | bytes 1572864 | tf_op jit(solution)/shard_map/reduce_scatter | solution.py:119
  17.4 6.0 %copy-start.15 = (bf16[8,16,1024]{2,1,0:T(8,128)(2,1)S(1)}, bf16[8,16,1024]{2,1,0:T(8,128)(2,1)}, u32[]{:S(2)}) copy-start(bf16[8,16,1024]{2,1,0:T(8,128)(2,1)} %param.14) | copy-start | bytes 786436
  23.4 14.1 %copy-start.10 = (bf16[256,8,64]{0,2,1:T(8,128)(2,1)}, bf16[256,8,64]{0,2,1:T(8,128)(2,1)S(1)}, u32[]{:S(2)}) copy-start(bf16[256,8,64]{0,2,1:T(8,128)(2,1)S(1)} %copy.102) | copy-start | bytes 786436
  23.4 1.8 copy-start.20
  24.8 1.1 copy-start.4
  24.8 1.1 copy-start.6
  25.9 11.5 %collective-permute-start.1 = (bf16[8,16,512]{2,1,0:T(8,128)(2,1)}, bf16[8,16,512]{2,1,0:T(8,128)(2,1)S(1)}, u32[]{:S(2)}, u32[]{:S(2)}) collective-permute-start(bf16[8,16,512]{2,1,0:T(8,128)(2,1)} %collective-permute-done), channel_id=1, source_target_pairs={{0,2},{2,4},{4,6},{6,8},{8,10},{10,12},{12,14},{14,0},{1,3},{3,5},... | collective-permute-start | bytes 393224 | tf_op jit(solution)/shard_map/ppermute | solution.py:19
  37.5 7.8 %copy-start.17 = (bf16[8,16,512]{2,1,0:T(8,128)(2,1)}, bf16[8,16,512]{2,1,0:T(8,128)(2,1)S(1)}, u32[]{:S(2)}) copy-start(bf16[8,16,512]{2,1,0:T(8,128)(2,1)S(1)} %collective-permute-done.1) | copy-start | bytes 393220
  37.5 7.8 %collective-permute-start.2 = (bf16[8,16,512]{2,1,0:T(8,128)(2,1)S(1)}, bf16[8,16,512]{2,1,0:T(8,128)(2,1)}, u32[]{:S(2)}, u32[]{:S(2)}) collective-permute-start(bf16[8,16,512]{2,1,0:T(8,128)(2,1)S(1)} %collective-permute-done.1), channel_id=1, source_target_pairs={{0,2},{2,4},{4,6},{6,8},{8,10},{10,12},{12,14},{14,0},{1,3},{3,5},... | collective-permute-start | bytes 393224 | tf_op jit(solution)/shard_map/ppermute | solution.py:19
  38.6 10.4 %collective-permute-start.5 = (bf16[8,16,512]{2,1,0:T(8,128)(2,1)}, bf16[8,16,512]{2,1,0:T(8,128)(2,1)S(1)}, u32[]{:S(2)}, u32[]{:S(2)}) collective-permute-start(bf16[8,16,512]{2,1,0:T(8,128)(2,1)} %collective-permute-done.4), channel_id=1, source_target_pairs={{0,14},{2,0},{4,2},{6,4},{8,6},{10,8},{12,10},{14,12},{1,15},{3,1}... | collective-permute-start | bytes 393224 | tf_op jit(solution)/shard_map/ppermute | solution.py:22
  45.3 10.8 %collective-permute-start.3 = (bf16[8,16,512]{2,1,0:T(8,128)(2,1)}, bf16[8,16,512]{2,1,0:T(8,128)(2,1)}, u32[]{:S(2)}, u32[]{:S(2)}) collective-permute-start(bf16[8,16,512]{2,1,0:T(8,128)(2,1)} %collective-permute-done.2), channel_id=1, source_target_pairs={{0,2},{2,4},{4,6},{6,8},{8,10},{10,12},{12,14},{14,0},{1,3},{3,5},... | collective-permute-start | bytes 393224 | tf_op jit(solution)/shard_map/ppermute | solution.py:19
  46.4 11.5 %copy-start.18 = (bf16[8,16,512]{2,1,0:T(8,128)(2,1)S(1)}, bf16[8,16,512]{2,1,0:T(8,128)(2,1)}, u32[]{:S(2)}) copy-start(bf16[8,16,512]{2,1,0:T(8,128)(2,1)} %copy-done.17) | copy-start | bytes 393220
  47.2 15.5 %copy-start.19 = (bf16[8,16,512]{2,1,0:T(8,128)(2,1)S(1)}, bf16[8,16,512]{2,1,0:T(8,128)(2,1)}, u32[]{:S(2)}) copy-start(bf16[8,16,512]{2,1,0:T(8,128)(2,1)} %copy-done.17) | copy-start | bytes 393220
  47.2 16.5 %copy-start.13 = (bf16[8,16,1024]{2,1,0:T(8,128)(2,1)S(1)}, bf16[8,16,1024]{2,1,0:T(8,128)(2,1)}, u32[]{:S(2)}) copy-start(bf16[8,16,1024]{2,1,0:T(8,128)(2,1)} %param.12) | copy-start | bytes 786436
  48.9 11.9 %collective-permute-start.6 = (bf16[8,16,512]{2,1,0:T(8,128)(2,1)S(1)}, bf16[8,16,512]{2,1,0:T(8,128)(2,1)S(1)}, u32[]{:S(2)}, u32[]{:S(2)}) collective-permute-start(bf16[8,16,512]{2,1,0:T(8,128)(2,1)S(1)} %collective-permute-done.5), channel_id=1, source_target_pairs={{0,14},{2,0},{4,2},{6,4},{8,6},{10,8},{12,10},{14,12},{1,15},{3,1}... | collective-permute-start | bytes 393224 | tf_op jit(solution)/shard_map/ppermute | solution.py:22
  58.0 9.3 %copy-start.12 = (bf16[128,8,64]{0,2,1:T(8,128)(2,1)S(1)}, bf16[128,8,64]{0,2,1:T(8,128)(2,1)}, u32[]{:S(2)}) copy-start(bf16[128,8,64]{0,2,1:T(8,128)(2,1)} %copy.104) | copy-start | bytes 393220
  63.7 1.4 copy-start.16
  68.4 0.8 copy-start.8
  71.3 126.5 %reduce-scatter.5.cloned.1.call-start = ((), (), s32[]{:S(2)}) async-start(), calls=%async_computation.4 | async-start | bytes 4718592 | tf_op jit(solution)/shard_map/reduce_scatter | solution.py:162
  76.7 3.3 %copy-start.2 = (bf16[2,64,8,64]{1,3,2,0:T(8,128)(2,1)}, bf16[2,64,8,64]{1,3,2,0:T(8,128)(2,1)S(1)}, u32[]{:S(2)}) copy-start(bf16[2,64,8,64]{1,3,2,0:T(8,128)(2,1)S(1)} %get-tuple-element.462) | copy-start | bytes 393220 | tf_op jit(solution)/shard_map/while
  84.9 2.4 %copy-start.1 = (bf16[1,32,16,512]{3,2,1,0:T(8,128)(2,1)S(1)}, bf16[1,32,16,512]{3,2,1,0:T(8,128)(2,1)}, u32[]{:S(2)}) copy-start(bf16[1,32,16,512]{3,2,1,0:T(8,128)(2,1)} %get-tuple-element.394) | copy-start | bytes 1572868 | tf_op jit(solution)/shard_map/while
  90.3 2.8 %copy-start = (f32[32,16,512]{2,1,0:T(8,128)S(1)}, f32[32,16,512]{2,1,0:T(8,128)}, u32[]{:S(2)}) copy-start(f32[32,16,512]{2,1,0:T(8,128)} %copy_bitcast_fusion.7) | copy-start | bytes 3145732 | tf_op jit(solution)/shard_map/while
  93.1 1.5 copy-start.3
  94.6 3.3 %copy-start.2 = (bf16[2,64,8,64]{1,3,2,0:T(8,128)(2,1)}, bf16[2,64,8,64]{1,3,2,0:T(8,128)(2,1)S(1)}, u32[]{:S(2)}) copy-start(bf16[2,64,8,64]{1,3,2,0:T(8,128)(2,1)S(1)} %get-tuple-element.462) | copy-start | bytes 393220 | tf_op jit(solution)/shard_map/while
  102.7 2.4 %copy-start.1 = (bf16[1,32,16,512]{3,2,1,0:T(8,128)(2,1)S(1)}, bf16[1,32,16,512]{3,2,1,0:T(8,128)(2,1)}, u32[]{:S(2)}) copy-start(bf16[1,32,16,512]{3,2,1,0:T(8,128)(2,1)} %get-tuple-element.394) | copy-start | bytes 1572868 | tf_op jit(solution)/shard_map/while
  108.2 2.8 %copy-start = (f32[32,16,512]{2,1,0:T(8,128)S(1)}, f32[32,16,512]{2,1,0:T(8,128)}, u32[]{:S(2)}) copy-start(f32[32,16,512]{2,1,0:T(8,128)} %copy_bitcast_fusion.7) | copy-start | bytes 3145732 | tf_op jit(solution)/shard_map/while
  111.0 1.5 copy-start.3
  112.5 1.0 copy-start.9
  112.5 1.1 copy-start.11
  112.5 2.5 %copy-start.5 = (bf16[2,64,8,64]{3,1,2,0:T(8,128)(2,1)S(1)}, bf16[2,64,8,64]{3,1,2,0:T(8,128)(2,1)}, u32[]{:S(2)}) copy-start(bf16[2,64,8,64]{3,1,2,0:T(8,128)(2,1)} %copy-done.4) | copy-start | bytes 393220
  118.0 1.0 copy-start.7
  122.7 1.0 copy-start.7
  124.3 1.0 copy-start.14
Sparse Core Ops, SparseCore 0:
  17.4 46.3 all-gather.1
Sparse Core Ops, SparseCore 1:
  71.4 5.8 reduce-scatter.2
  112.6 85.1 reduce-scatter.4
